TPU v7x, 512 devices: a whole 4x4x16 slice. The times are simulated.
512 devices in a mesh: page: 16 (over z), blk: 32 (over y, x, core).
Axes of the slice: x: 4, y: 4, z: 16, core: 2. Of those that a mesh axis runs over, the one named last changes fastest.
Arguments:
- queries: bfloat16 [64, 2, 32, 128], P(None, None, 'blk'), may hold values from -192 to 192
- prompt_kv: bfloat16 [256, 64, 32, 256], P('page', None, 'blk'), may hold values from -36 to 36
- tail_kv: bfloat16 [64, 256, 32, 256], P('page', None, 'blk'), may hold values from -36 to 36
- page_table: int32 [4, 64], replicated, may hold values from 0 to 255, as said below
- prompt_len: int32 [4], replicated, may hold values from 1 to 4096, 10240 in all
- tail_len: int32 [64], replicated, may hold values from 0 to 254, as said below
- sample_prompt: int32 [64], replicated, may hold values from 0 to 3, as said below
- stream_in: bfloat16 [64, 2, 7168], P(None, None, 'blk'), may hold values from -6 to 6
- w_out: bfloat16 [4096, 7168], P('blk'), may hold values from -0.09375 to 0.09375
- b_out: bfloat16 [7168], replicated, may hold values from -3 to 3
- ln_gain: bfloat16 [7168], P('page'), may hold values from 0.25 to 1.75
- ln_bias: bfloat16 [7168], P('page'), may hold values from -3 to 3
- w_up: bfloat16 [7168, 28672], P('page', 'blk'), may hold values from -0.0625 to 0.0625
- b_up: bfloat16 [28672], P('blk'), may hold values from -3 to 3
- w_down: bfloat16 [28672, 7168], P('blk', 'page'), may hold values from -0.046875 to 0.046875
- b_down: bfloat16 [7168], P(('page', 'blk')), may hold values from -3 to 3
- w_score: bfloat16 [7168], P(('page', 'blk')), may hold values from -0.0625 to 0.0625
Outputs:
- layer_output: bfloat16 [64, 2, 7168], P(None, None, ('page', 'blk'))
- sample_score: float32 [64, 2], replicated
Inputs may be any that keep to these rules, and one draw needn't show every extreme that they name: `page_table`: every slot number appears exactly once in the table. `tail_len`: some sample reaches the largest value. `sample_prompt`: each prompt has exactly 16 samples.
All inputs are finite; a program needn't handle non-finite values.
Results may differ from a plain program's by a relative error of at most 0.03.
Values may be sent and summed in bfloat16 or wider, within the bound.
A program may use at most 64 MiB of HBM per device.

v0:
```python
import math
import jax
import jax.numpy as jnp
from jax import lax
from jax.sharding import PartitionSpec as P

NEGATIVE = -1e30


def combined_all(value, axis, join):
    pieces = jax.tree.map(lambda part: lax.all_gather(part, axis), value)
    head = jax.tree.map(lambda part: part[0], pieces)
    tail = jax.tree.map(lambda part: part[1:], pieces)
    subtotal, _ = lax.scan(lambda subtotal, share: (join(subtotal, share), None), head, tail)
    return subtotal


def join_partials(earlier, later):
    highest = jnp.maximum(earlier[0], later[0])
    left_scale = jnp.exp(earlier[0] - highest)
    right_scale = jnp.exp(later[0] - highest)
    return (
        highest,
        earlier[1] * left_scale + later[1] * right_scale,
        earlier[2] * left_scale[..., None] + later[2] * right_scale[..., None],
    )


def softmax_part(scores, visible):
    masked = jnp.where(visible, scores, NEGATIVE)
    highest = jnp.max(masked, axis=-1)
    weights = jnp.where(visible, jnp.exp(scores - highest[..., None]), 0.0)
    return (highest, jnp.sum(weights, axis=-1), weights.astype(jnp.bfloat16))


def body(
    queries,
    prompt_kv,
    tail_kv,
    page_table,
    prompt_len,
    tail_len,
    sample_prompt,
    stream_in,
    w_out,
    b_out,
    ln_gain,
    ln_bias,
    w_up,
    b_up,
    w_down,
    b_down,
    w_score,
):
    samples, new_count, heads_dev, head_dim = queries.shape
    slots_dev, page_len = (prompt_kv.shape[0], prompt_kv.shape[1])
    own_count, tail_max = (tail_kv.shape[0], tail_kv.shape[1])
    prompts, pages_max = page_table.shape
    page_pos = lax.axis_index("page")
    blk_pos = lax.axis_index("blk")
    inv_sqrt = 1.0 / math.sqrt(head_dim)
    entries = page_table.reshape(-1)
    slot_ids = page_pos * slots_dev + jnp.arange(slots_dev, dtype=jnp.int32)
    matched = (entries[:, None] == slot_ids[None, :]).astype(jnp.int32)
    owner_index = jnp.sum(matched * jnp.arange(entries.shape[0], dtype=jnp.int32)[:, None], axis=0)
    slot_prompt = owner_index // pages_max
    slot_page = owner_index % pages_max
    prompt_pick = (slot_prompt[:, None] == jnp.arange(prompts, dtype=jnp.int32)[None, :]).astype(
        jnp.int32
    )
    slot_limit = jnp.sum(prompt_pick * prompt_len[None, :], axis=1)
    key_pos = slot_page[:, None] * page_len + jnp.arange(page_len, dtype=jnp.int32)[None, :]
    key_live = (key_pos < slot_limit[:, None]).reshape(-1)
    key_prompt = jnp.repeat(slot_prompt, page_len)
    prompt_visible = ((sample_prompt[:, None] == key_prompt[None, :]) & key_live[None, :])[
        :, None, None, :
    ]
    cache_rows = prompt_kv.reshape(slots_dev * page_len, heads_dev, 2 * head_dim)
    prompt_scores = (
        jnp.einsum(
            "snhd,khd->snhk",
            queries,
            cache_rows[:, :, :head_dim],
            preferred_element_type=jnp.float32,
        )
        * inv_sqrt
    )
    high_p, sum_p, weights_p = softmax_part(prompt_scores, prompt_visible)
    mixed_p = jnp.einsum(
        "snhk,khd->snhd", weights_p, cache_rows[:, :, head_dim:], preferred_element_type=jnp.float32
    )
    first_row = page_pos * own_count
    own_queries = lax.dynamic_slice_in_dim(queries, first_row, own_count, 0)
    own_lengths = lax.dynamic_slice_in_dim(tail_len, first_row, own_count, 0)
    tail_scores = (
        jnp.einsum(
            "snhd,sthd->snht",
            own_queries,
            tail_kv[..., :head_dim],
            preferred_element_type=jnp.float32,
        )
        * inv_sqrt
    )
    reach_pos = own_lengths[:, None] + jnp.arange(new_count, dtype=jnp.int32)[None, :]
    tail_visible = (
        jnp.arange(tail_max, dtype=jnp.int32)[None, None, None, :] <= reach_pos[:, :, None, None]
    )
    high_t, sum_t, weights_t = softmax_part(tail_scores, tail_visible)
    mixed_t = jnp.einsum(
        "snht,sthd->snhd", weights_t, tail_kv[..., head_dim:], preferred_element_type=jnp.float32
    )
    high_t = lax.dynamic_update_slice_in_dim(
        jnp.full(high_p.shape, NEGATIVE, jnp.float32), high_t, first_row, 0
    )
    sum_t = lax.dynamic_update_slice_in_dim(
        jnp.zeros(sum_p.shape, jnp.float32), sum_t, first_row, 0
    )
    mixed_t = lax.dynamic_update_slice_in_dim(
        jnp.zeros(mixed_p.shape, jnp.float32), mixed_t, first_row, 0
    )
    partial_value = join_partials((high_p, sum_p, mixed_p), (high_t, sum_t, mixed_t))
    merged = combined_all(partial_value, "page", join_partials)
    weight_sum, weighted = (merged[1], merged[2])
    attention = (
        (weighted / weight_sum[..., None])
        .astype(jnp.bfloat16)
        .reshape(samples * new_count, heads_dev * head_dim)
    )
    contrib = jnp.dot(attention, w_out, preferred_element_type=jnp.float32)
    slice_width = stream_in.shape[2]
    column = blk_pos * slice_width
    own_stream = stream_in.reshape(samples * new_count, slice_width).astype(jnp.float32)
    contrib = lax.dynamic_update_slice_in_dim(
        contrib, lax.dynamic_slice_in_dim(contrib, column, slice_width, 1) + own_stream, column, 1
    )
    summed = lax.psum(contrib, "blk")
    residual = (summed + b_out.astype(jnp.float32)).astype(jnp.bfloat16)
    residual_f = residual.astype(jnp.float32)
    row_mean = jnp.mean(residual_f, axis=-1, keepdims=True)
    centred = residual_f - row_mean
    inverse_std = lax.rsqrt(jnp.mean(centred * centred, axis=-1, keepdims=True) + 1e-05)
    feature_count = ln_gain.shape[0]
    first_col = page_pos * feature_count
    normed = (
        lax.dynamic_slice_in_dim(centred, first_col, feature_count, 1)
        * inverse_std
        * ln_gain.astype(jnp.float32)
        + ln_bias.astype(jnp.float32)
    ).astype(jnp.bfloat16)
    up_part = jnp.dot(normed, w_up, preferred_element_type=jnp.float32).astype(jnp.bfloat16)
    hidden_sum = lax.psum(up_part, "page").astype(jnp.float32)
    hidden = jnp.maximum(hidden_sum + b_up.astype(jnp.float32), 0.0).astype(jnp.bfloat16)
    projected = jnp.dot(hidden, w_down, preferred_element_type=jnp.float32)
    out_share = lax.psum_scatter(projected, "blk", scatter_dimension=1, tiled=True)
    piece_width = b_down.shape[0]
    out_column = first_col + blk_pos * piece_width
    output = (
        out_share
        + lax.dynamic_slice_in_dim(residual_f, out_column, piece_width, 1)
        + b_down.astype(jnp.float32)
    ).astype(jnp.bfloat16)
    score_part = jnp.sum(output.astype(jnp.float32) * w_score.astype(jnp.float32), axis=-1)
    row_score = lax.psum(score_part, ("page", "blk"))
    return (output.reshape(samples, new_count, piece_width), row_score.reshape(samples, new_count))


def solution(mesh):
    placed = (
        P(None, None, "blk", None),
        P("page", None, "blk", None),
        P("page", None, "blk", None),
        P(),
        P(),
        P(),
        P(),
        P(None, None, "blk"),
        P("blk", None),
        P(),
        P("page"),
        P("page"),
        P("page", "blk"),
        P("blk"),
        P("blk", "page"),
        P(("page", "blk")),
        P(("page", "blk")),
    )
    return jax.shard_map(
        body,
        mesh=mesh,
        in_specs=placed,
        out_specs=(P(None, None, ("page", "blk")), P()),
        check_vma=False,
    )
```

profile of v0, /device:TPU:1, one launch (start us, length us, event | category | flops | bytes accessed | tf_op | source)
XLA Modules:
  0.0 637.5 jit_solution(366933933234473874)
XLA Ops:
  7.2 0.9 dynamic_slice.26
  8.2 1.2 select_reduce_fusion.2
  9.7 1.2 fusion.14
  10.9 0.8 eq.50
  11.9 0.7 select_reduce_fusion.3
  13.2 0.8 compare_and_fusion
  14.0 1.3 select_reduce_fusion
  15.2 0.3 fusion.11
  15.5 1.9 fusion.8
  17.6 33.1 %all-gather = f32[1024,2,1]{1,2,0:T(1,128)S(1)} all-gather(f32[64,2,1]{1,2,0:T(1,128)S(1)} %copy.76), channel_id=2, replica_groups=mesh['page'=16,'blk'=32] {'page'}, dimensions={0}, use_global_device_ids=true | all-gather | bytes 8704 | tf_op jit(solution)/shard_map/all_gather | solution.py:11
  50.9 25.1 %all-gather.1 = f32[1024,2,1]{1,2,0:T(1,128)S(1)} all-gather(f32[64,2,1]{1,2,0:T(1,128)S(1)} %copy.78), channel_id=3, replica_groups=mesh['page'=16,'blk'=32] {'page'}, dimensions={0}, use_global_device_ids=true | all-gather | bytes 8704 | tf_op jit(solution)/shard_map/all_gather | solution.py:11
  76.2 0.2 copy.87
  76.7 8.9 %all-gather.5.cloned.1.call-done = f32[1024,2,1,128]{3,0,1,2:T(8,128)} async-done(((f32[64,2,1,128]{3,0,1,2:T(8,128)}), f32[1024,2,1,128]{3,0,1,2:T(8,128)}) %all-gather.5.cloned.1.call-update) | async-done | bytes 1048592 | tf_op jit(solution)/shard_map/all_gather | solution.py:11
  85.6 0.8 slice.52
  86.5 1.3 slice.55
  87.7 10.6 %while.14 = (s32[]{:T(128)}, f32[64,2,1]{0,1,2:T(2,128)S(1)}, f32[64,2,1]{0,1,2:T(2,128)S(1)}, f32[64,2,1,128]{3,2,1,0:T(1,128)S(1)}, f32[15,64,2,1]{1,2,3,0:T(2...) while((s32[]{:T(128)}, f32[64,2,1]{0,1,2:T(2,128)S(1)}, ...), condition=%wide.region_7.8_spmd, body=%wide.region_6.7_spmd.sunk | while | flops 50050 | bytes 468577 | solution.py:14
  88.1 0.4 multiply_add_fusion.2
  88.8 0.4 multiply_add_fusion.2
  89.5 0.4 multiply_add_fusion.2
  90.2 0.4 multiply_add_fusion.2
  90.9 0.4 multiply_add_fusion.2
  91.6 0.4 multiply_add_fusion.2
  92.3 0.4 multiply_add_fusion.2
  93.0 0.4 multiply_add_fusion.2
  93.7 0.4 multiply_add_fusion.2
  94.4 0.4 multiply_add_fusion.2
  95.1 0.4 multiply_add_fusion.2
  95.8 0.4 multiply_add_fusion.2
  96.5 0.4 multiply_add_fusion.2
  97.2 0.4 multiply_add_fusion.2
  97.9 0.4 multiply_add_fusion.2
  98.4 0.2 divide_convert_fusion
  98.7 0.6 fusion.44
  99.4 1.8 copy-done.1
  101.3 1.9 dynamic_update_slice.15
  103.3 147.2 %all-reduce.5.cloned.1.call-done = f32[128,7168]{1,0:T(8,128)} async-done(((f32[128,7168]{1,0:T(8,128)}), f32[128,7168]{1,0:T(8,128)}) %all-reduce.5.cloned.1.call-update) | async-done | bytes 3670032 | tf_op jit(solution)/shard_map/psum | solution.py:136
  250.5 2.5 fusion.42
  253.1 0.8 multiply_reduce_fusion
  253.9 1.0 copy-done.2
  254.9 1.1 convolution_convert_fusion
  256.1 126.2 %all-reduce.7.cloned.1.call-done = bf16[128,896]{1,0:T(8,128)(2,1)} async-done(((bf16[128,896]{1,0:T(8,128)(2,1)}), bf16[128,896]{1,0:T(8,128)(2,1)}) %all-reduce.7.cloned.1.call-update) | async-done | bytes 229392 | tf_op jit(solution)/shard_map/psum | solution.py:151
  382.3 2.0 fusion.18
  384.4 1.3 dynamic-slice
  386.3 137.0 %all-reduce.9.cloned.1.call-done = f32[128,448]{1,0:T(8,128)} async-done(((f32[128,448]{1,0:T(8,128)}), f32[128,448]{1,0:T(8,128)}) %all-reduce.9.cloned.1.call-update) | async-done | bytes 229392
  523.3 1.1 multiply_reduce_fusion.1
  524.6 105.0 %psum.23 = f32[64,2]{1,0:T(8,128)S(1)} all-reduce(f32[64,2]{1,0:T(8,128)S(1)} %reshape.251), channel_id=1, replica_groups=mesh['page'=16,'blk'=32] {'page','blk'}, use_global_device_ids=true, to_apply=%region_14.15 | all-reduce | flops 128 | bytes 1024 | tf_op jit(solution)/shard_map/psum | solution.py:163
  629.6 0.6 copy.92
  630.3 0.7 copy.91
  (176 shorter events, 7.0 us)
Async XLA Ops:
  7.2 91.5 %copy-start = (bf16[128,7168]{1,0:T(8,128)(2,1)S(1)}, bf16[128,7168]{1,0:T(8,128)(2,1)}, u32[]{:S(2)}) copy-start(bf16[128,7168]{1,0:T(8,128)(2,1)} %param.27) | copy-start | bytes 5505028
  7.2 78.4 %all-gather.5.cloned.1.call-start = ((), (), s32[]{:S(2)}) async-start(), calls=%async_computation.2 | async-start | bytes 1114112 | tf_op jit(solution)/shard_map/all_gather | solution.py:11
  12.7 63.9 %copy-start.5 = (bf16[64,2,224]{2,1,0:T(2,128)(2,1)S(1)}, bf16[64,2,224]{2,1,0:T(2,128)(2,1)}, u32[]{:S(2)}) copy-start(bf16[64,2,224]{2,1,0:T(2,128)(2,1)} %param.26) | copy-start | bytes 172036
  17.4 233.1 %all-reduce.5.cloned.1.call-start = ((), (), s32[]{:S(2)}) async-start(), calls=%async_computation | async-start | bytes 7340032 | tf_op jit(solution)/shard_map/psum | solution.py:136
  98.7 4.6 copy-start.6
  98.7 4.6 copy-start.8
  98.7 4.6 copy-start.9
  99.3 1.8 copy-start.1
  103.2 279.1 %all-reduce.7.cloned.1.call-start = ((), (), s32[]{:S(2)}) async-start(), calls=%async_computation.1 | async-start | bytes 458752 | tf_op jit(solution)/shard_map/psum | solution.py:151
  253.0 1.9 copy-start.2
  253.1 1.9 copy-start.4
  253.1 3.0 copy-start.7
  253.1 129.2 %copy-start.3 = (bf16[896,448]{0,1:T(8,128)(2,1)S(1)}, bf16[896,448]{0,1:T(8,128)(2,1)}, u32[]{:S(2)}) copy-start(bf16[896,448]{0,1:T(8,128)(2,1)} %param.33) | copy-start | bytes 2408452
  253.1 131.3 %copy-start.10 = (bf16[14]{0:T(256)(128)(2,1)S(1)}, bf16[14]{0:T(256)(128)(2,1)}, u32[]{:S(2)}) copy-start(bf16[14]{0:T(256)(128)(2,1)} %param.34) | copy-start | bytes 88
  253.1 131.3 %copy-start.11 = (bf16[14]{0:T(256)(128)(2,1)S(1)}, bf16[14]{0:T(256)(128)(2,1)}, u32[]{:S(2)}) copy-start(bf16[14]{0:T(256)(128)(2,1)} %param.35) | copy-start | bytes 88
  256.0 267.3 %all-reduce.9.cloned.1.call-start = ((), (), s32[]{:S(2)}) async-start(), calls=%async_computation.3 | async-start | bytes 524288
Sparse Core Ops, SparseCore 0:
  17.6 67.9 all-gather.4
  103.3 147.1 all-reduce.4
  256.2 126.0 all-reduce.6
  385.7 137.5 all-reduce.8
where the time goes:
time: 638 us; the launch traced here: 637 us
  waiting for transfers between devices  419 us (66%)
  blocking collectives  163 us (26%)
  local copies, waits for them, and re-layouts  16.8 us (3%)
  between operations  14.8 us (2%)
  other arithmetic  13.4 us (2%)
  matrix products  9.27 us (1%)
    psum x1, waiting for transfers between devices, body(): summed = lax.psum(contrib, 'blk')  147 us
    unnamed x5, waiting for transfers between devices  137 us
    psum x1, waiting for transfers between devices, body(): hidden_sum = lax.psum(up_part, 'page').astype(jnp.float32)  126 us
    psum x1, blocking collectives, body(): row_score = lax.psum(score_part, ('page', 'blk'))  105 us
    all_gather x2, blocking collectives, combined_all(): pieces = jax.tree.map(lambda part: lax.all_gather(part, axis), value)  58.2 us
  transfers between devices with their start and end apart: 4, of which 4 were waited for; matrix products, arithmetic and copies ran while one was open for 0% of the time, Pallas kernels for 0%

commit v1 on v0

--- a/solution.py
+++ b/solution.py
@@ -148,7 +148,7 @@
         + ln_bias.astype(jnp.float32)
     ).astype(jnp.bfloat16)
     up_part = jnp.dot(normed, w_up, preferred_element_type=jnp.float32).astype(jnp.bfloat16)
-    hidden_sum = lax.psum(up_part, "page").astype(jnp.float32)
+    hidden_sum = jnp.sum(lax.all_gather(up_part, "page"), axis=0).astype(jnp.float32)
     hidden = jnp.maximum(hidden_sum + b_up.astype(jnp.float32), 0.0).astype(jnp.bfloat16)
     projected = jnp.dot(hidden, w_down, preferred_element_type=jnp.float32)
     out_share = lax.psum_scatter(projected, "blk", scatter_dimension=1, tiled=True)

time: 638 us -> 581 us (0.911)
  waiting for transfers between devices: 419 us -> 361 us
    psum x1 -> x0, waiting for transfers between devices: 126 us -> none  [body(): hidden_sum = lax.psum(up_part, 'page').astype(jnp.float32)]
    all_gather x0 -> x1, waiting for transfers between devices: none -> 69 us  [body(): lax.all_gather(up_part, 'page')]
where the time goes in v1:
time: 581 us; the launch traced here: 580 us
  waiting for transfers between devices  361 us (62%)
  blocking collectives  163 us (28%)
  local copies, waits for them, and re-layouts  16.7 us (3%)
  other arithmetic  16 us (3%)
  between operations  14.8 us (3%)
  matrix products  8.33 us (1%)
    psum x1, waiting for transfers between devices, body(): summed = lax.psum(contrib, 'blk')  147 us
    unnamed x5, waiting for transfers between devices  136 us
    psum x1, blocking collectives, body(): row_score = lax.psum(score_part, ('page', 'blk'))  105 us
    all_gather x1, waiting for transfers between devices, body(): lax.all_gather(up_part, 'page')  69 us
    all_gather x2, blocking collectives, combined_all(): pieces = jax.tree.map(lambda part: lax.all_gather(part, axis), value)  58.2 us
  transfers between devices with their start and end apart: 4, of which 4 were waited for; matrix products, arithmetic and copies ran while one was open for 0% of the time, Pallas kernels for 0%

profile of v1, /device:TPU:1, one launch (start us, length us, event | category | flops | bytes accessed | tf_op | source)
XLA Modules:
  0.0 580.4 jit_solution(5242662359437724192)
XLA Ops:
  7.2 0.9 dynamic_slice.26
  8.2 1.2 select_reduce_fusion.2
  9.7 1.2 fusion.14
  10.9 0.8 eq.50
  11.9 0.7 select_reduce_fusion.3
  13.2 0.8 compare_and_fusion
  14.0 1.3 select_reduce_fusion
  15.2 0.3 fusion.11
  15.5 1.9 fusion.8
  17.6 33.1 %all-gather = f32[1024,2,1]{1,2,0:T(1,128)S(1)} all-gather(f32[64,2,1]{1,2,0:T(1,128)S(1)} %copy.76), channel_id=2, replica_groups=mesh['page'=16,'blk'=32] {'page'}, dimensions={0}, use_global_device_ids=true | all-gather | bytes 8704 | tf_op jit(solution)/shard_map/all_gather | solution.py:11
  50.9 25.1 %all-gather.1 = f32[1024,2,1]{1,2,0:T(1,128)S(1)} all-gather(f32[64,2,1]{1,2,0:T(1,128)S(1)} %copy.78), channel_id=3, replica_groups=mesh['page'=16,'blk'=32] {'page'}, dimensions={0}, use_global_device_ids=true | all-gather | bytes 8704 | tf_op jit(solution)/shard_map/all_gather | solution.py:11
  76.2 0.2 copy.87
  76.7 8.9 %all-gather.7.cloned.1.call-done = f32[1024,2,1,128]{3,0,1,2:T(8,128)} async-done(((f32[64,2,1,128]{3,0,1,2:T(8,128)}), f32[1024,2,1,128]{3,0,1,2:T(8,128)}) %all-gather.7.cloned.1.call-update) | async-done | bytes 1048592 | tf_op jit(solution)/shard_map/all_gather | solution.py:11
  85.6 0.8 slice.52
  86.5 1.3 slice.55
  87.7 10.6 %while.14 = (s32[]{:T(128)}, f32[64,2,1]{0,1,2:T(2,128)S(1)}, f32[64,2,1]{0,1,2:T(2,128)S(1)}, f32[64,2,1,128]{3,2,1,0:T(1,128)S(1)}, f32[15,64,2,1]{1,2,3,0:T(2...) while((s32[]{:T(128)}, f32[64,2,1]{0,1,2:T(2,128)S(1)}, ...), condition=%wide.region_7.8_spmd, body=%wide.region_6.7_spmd.sunk | while | flops 50050 | bytes 468577 | solution.py:14
  88.1 0.4 multiply_add_fusion.2
  88.8 0.4 multiply_add_fusion.2
  89.5 0.4 multiply_add_fusion.2
  90.2 0.4 multiply_add_fusion.2
  90.9 0.4 multiply_add_fusion.2
  91.6 0.4 multiply_add_fusion.2
  92.3 0.4 multiply_add_fusion.2
  93.0 0.4 multiply_add_fusion.2
  93.7 0.4 multiply_add_fusion.2
  94.4 0.4 multiply_add_fusion.2
  95.1 0.4 multiply_add_fusion.2
  95.8 0.4 multiply_add_fusion.2
  96.5 0.4 multiply_add_fusion.2
  97.2 0.4 multiply_add_fusion.2
  97.9 0.4 multiply_add_fusion.2
  98.7 0.6 fusion.44
  99.4 1.8 copy-done.1
  101.3 1.9 dynamic_update_slice.15
  103.3 147.2 %all-reduce.4.cloned.1.call-done = f32[128,7168]{1,0:T(8,128)} async-done(((f32[128,7168]{1,0:T(8,128)}), f32[128,7168]{1,0:T(8,128)}) %all-reduce.4.cloned.1.call-update) | async-done | bytes 3670032 | tf_op jit(solution)/shard_map/psum | solution.py:136
  250.5 2.5 fusion.42
  253.1 0.8 multiply_reduce_fusion
  253.9 1.0 copy-done.2
  254.9 1.1 convolution_convert_fusion
  256.0 69.0 %all-gather.9.cloned.1.call-done = bf16[2048,896]{1,0:T(8,128)(2,1)} async-done(((bf16[128,896]{1,0:T(8,128)(2,1)}), bf16[2048,896]{1,0:T(8,128)(2,1)}) %all-gather.9.cloned.1.call-update) | async-done | bytes 3670032 | tf_op jit(solution)/shard_map/all_gather | solution.py:151
  325.0 2.6 reduce_sum.87
  327.6 1.1 fusion.18
  328.8 1.3 dynamic-slice
  330.7 135.5 %all-reduce.6.cloned.1.call-done = f32[128,448]{1,0:T(8,128)} async-done(((f32[128,448]{1,0:T(8,128)}), f32[128,448]{1,0:T(8,128)}) %all-reduce.6.cloned.1.call-update) | async-done | bytes 229392
  466.3 1.1 multiply_reduce_fusion.1
  467.6 105.0 %psum.15 = f32[64,2]{1,0:T(8,128)S(1)} all-reduce(f32[64,2]{1,0:T(8,128)S(1)} %reshape.251), channel_id=1, replica_groups=mesh['page'=16,'blk'=32] {'page','blk'}, use_global_device_ids=true, to_apply=%region_14.15 | all-reduce | flops 128 | bytes 1024 | tf_op jit(solution)/shard_map/psum | solution.py:163
  572.6 0.6 copy.92
  573.2 0.7 copy.91
  (177 shorter events, 7.2 us)
Async XLA Ops:
  7.2 91.5 %copy-start = (bf16[128,7168]{1,0:T(8,128)(2,1)S(1)}, bf16[128,7168]{1,0:T(8,128)(2,1)}, u32[]{:S(2)}) copy-start(bf16[128,7168]{1,0:T(8,128)(2,1)} %param.27) | copy-start | bytes 5505028
  7.2 78.4 %all-gather.7.cloned.1.call-start = ((), (), s32[]{:S(2)}) async-start(), calls=%async_computation.1 | async-start | bytes 1114112 | tf_op jit(solution)/shard_map/all_gather | solution.py:11
  12.7 63.9 %copy-start.5 = (bf16[64,2,224]{2,1,0:T(2,128)(2,1)S(1)}, bf16[64,2,224]{2,1,0:T(2,128)(2,1)}, u32[]{:S(2)}) copy-start(bf16[64,2,224]{2,1,0:T(2,128)(2,1)} %param.26) | copy-start | bytes 172036
  17.4 233.1 %all-reduce.4.cloned.1.call-start = ((), (), s32[]{:S(2)}) async-start(), calls=%async_computation | async-start | bytes 7340032 | tf_op jit(solution)/shard_map/psum | solution.py:136
  98.7 4.6 copy-start.6
  98.7 4.6 copy-start.8
  98.7 4.6 copy-start.9
  99.3 1.8 copy-start.1
  103.2 221.8 %all-gather.9.cloned.1.call-start = ((), (), s32[]{:S(2)}) async-start(), calls=%async_computation.2 | async-start | bytes 3899392 | tf_op jit(solution)/shard_map/all_gather | solution.py:151
  253.0 1.8 copy-start.2
  253.1 1.8 copy-start.4
  253.1 2.9 copy-start.7
  254.9 72.8 %copy-start.3 = (bf16[896,448]{0,1:T(8,128)(2,1)S(1)}, bf16[896,448]{0,1:T(8,128)(2,1)}, u32[]{:S(2)}) copy-start(bf16[896,448]{0,1:T(8,128)(2,1)} %param.33) | copy-start | bytes 2408452
  254.9 73.9 %copy-start.10 = (bf16[14]{0:T(256)(128)(2,1)S(1)}, bf16[14]{0:T(256)(128)(2,1)}, u32[]{:S(2)}) copy-start(bf16[14]{0:T(256)(128)(2,1)} %param.34) | copy-start | bytes 88
  254.9 73.9 %copy-start.11 = (bf16[14]{0:T(256)(128)(2,1)S(1)}, bf16[14]{0:T(256)(128)(2,1)}, u32[]{:S(2)}) copy-start(bf16[14]{0:T(256)(128)(2,1)} %param.35) | copy-start | bytes 88
  256.0 210.3 %all-reduce.6.cloned.1.call-start = ((), (), s32[]{:S(2)}) async-start(), calls=%async_computation.3 | async-start | bytes 524288
Sparse Core Ops, SparseCore 0:
  17.6 67.9 all-gather.6
  103.3 147.1 all-reduce.3
  256.1 68.8 all-gather.8
  328.9 137.3 all-reduce.5
